TPU v7x, 32 devices: a whole 2x2x4 slice. The times are simulated.
32 devices in a mesh: seq: 8 (over z, y), head: 4 (over x, core).
Axes of the slice: x: 2, y: 2, z: 4, core: 2. Of those that a mesh axis runs over, the one named last changes fastest.
Arguments:
- tokens: bfloat16 [1024, 2048], P('seq'), may hold values from -20 to 20, as said below
- projection: bfloat16 [2048, 3072], P(None, 'head'), may hold values from -0.078125 to 0.078125
- context_cotangent: bfloat16 [1024, 2048], P('seq', 'head'), may hold values from -80 to 80
Outputs:
- perturbed_context: bfloat16 [1024, 2048], P('seq', 'head')
- ascent_direction: float32 [2048, 3072], P('seq', 'head')
Inputs may be any that keep to these rules, and one draw needn't show every extreme that they name: `tokens`: activations of the layer.
All inputs are finite; a program needn't handle non-finite values.
Results may differ from a plain program's by a relative error of at most 0.017.
Values may be sent and summed in bfloat16 or wider, within the bound.
A program may use at most 64 MiB of HBM per device.

v0:
```python
import math
import jax
import jax.numpy as jnp
from jax import lax
from jax.sharding import PartitionSpec as P

INPUT_FEATURES = 2048
KEY_VALUE_HEADS = 4
HEAD_DIMENSION = 128
QUERY_PER_GROUP = 4
masked_score = -1e30
key_block = 512


def attend_fold(query_rows, query_pos, score_scale):
    head_size = query_rows.shape[1]

    def single_block(carry_state, block_rows, offset):
        running_max, row_total, context_sum = carry_state
        key_rows = block_rows[:, :head_size]
        value_rows = block_rows[:, head_size:].astype(jnp.float32)
        scores = jnp.dot(query_rows, key_rows.T, preferred_element_type=jnp.float32) * score_scale
        key_pos = offset + jnp.arange(block_rows.shape[0], dtype=jnp.int32)
        allowed = key_pos[None, :] <= query_pos[:, None]
        scores = jnp.where(allowed, scores, masked_score)
        new_max = jnp.maximum(running_max, jnp.max(scores, axis=1))
        factor = jnp.exp(running_max - new_max)
        weights = jnp.where(allowed, jnp.exp(scores - new_max[:, None]), 0.0)
        row_total = row_total * factor + jnp.sum(weights, axis=1)
        context_sum = context_sum * factor[:, None] + jnp.dot(
            weights, value_rows, precision=lax.Precision.HIGHEST, preferred_element_type=jnp.float32
        )
        return (new_max, row_total, context_sum)

    def fold_keys(carry_state, block_rows, offset):
        row_count = block_rows.shape[0]
        if row_count > key_block and row_count % key_block == 0:

            def sub_block(block_index, inner_state):
                part_rows = lax.dynamic_slice_in_dim(
                    block_rows, block_index * key_block, key_block, 0
                )
                return single_block(inner_state, part_rows, block_index * key_block)

            return lax.fori_loop(0, row_count // key_block, sub_block, carry_state)
        return single_block(carry_state, block_rows, offset)

    return fold_keys


def on_device(tokens, projection, context_cotangent):
    score_scale = HEAD_DIMENSION ** (-0.5)
    local_rows = tokens.shape[0]
    rows_all = local_rows * QUERY_PER_GROUP
    first_row = lax.axis_index("seq") * local_rows
    query_pos = first_row + jnp.arange(rows_all, dtype=jnp.int32) // QUERY_PER_GROUP

    def split_heads(projected_weight):
        reshaped_grads = projected_weight.reshape(local_rows, QUERY_PER_GROUP + 2, HEAD_DIMENSION)
        query_rows = reshaped_grads[:, :QUERY_PER_GROUP].reshape(rows_all, HEAD_DIMENSION)
        key_value = reshaped_grads[:, QUERY_PER_GROUP:].reshape(local_rows, 2 * HEAD_DIMENSION)
        return (query_rows, key_value)

    def empty_state():
        return (
            jnp.full((rows_all,), masked_score, jnp.float32),
            jnp.zeros((rows_all,), jnp.float32),
            jnp.zeros((rows_all, HEAD_DIMENSION), jnp.float32),
        )

    projected_weight = jnp.dot(tokens, projection, preferred_element_type=jnp.float32).astype(
        jnp.bfloat16
    )
    query_rows, key_value = split_heads(projected_weight)
    gathered = lax.all_gather(key_value, "seq", axis=0, tiled=True)
    total_rows = gathered.shape[0]
    block_size = min(key_block, total_rows)
    needed = (first_row + local_rows - 1) // block_size + 1
    fold_first = attend_fold(query_rows, query_pos, score_scale)

    def forward_step(block_index, carry_state):
        block_rows = lax.dynamic_slice_in_dim(gathered, block_index * block_size, block_size, 0)
        return fold_first(carry_state, block_rows, block_index * block_size)

    running_max, row_total, context_sum = lax.fori_loop(0, needed, forward_step, empty_state())
    context = (context_sum / row_total[:, None]).astype(jnp.bfloat16)
    log_total = running_max + jnp.log(row_total)
    grad_rows = context_cotangent.reshape(rows_all, HEAD_DIMENSION)
    row_delta = jnp.sum(grad_rows.astype(jnp.float32) * context.astype(jnp.float32), axis=1)
    contract_rows = (((0,), (0,)), ((), ()))

    def backward_step(block_index, carry_state):
        query_grad, key_terms = carry_state
        offset = block_index * block_size
        block_rows = lax.dynamic_slice_in_dim(gathered, offset, block_size, 0)
        key_rows = block_rows[:, :HEAD_DIMENSION]
        value_rows = block_rows[:, HEAD_DIMENSION:]
        scores = jnp.dot(query_rows, key_rows.T, preferred_element_type=jnp.float32) * score_scale
        key_pos = offset + jnp.arange(block_size, dtype=jnp.int32)
        allowed = key_pos[None, :] <= query_pos[:, None]
        probs_full = jnp.where(allowed, jnp.exp(scores - log_total[:, None]), 0.0)
        probs_half = probs_full.astype(jnp.bfloat16)
        prob_grad = jnp.dot(grad_rows, value_rows.T, preferred_element_type=jnp.float32)
        score_grad = (probs_full * (prob_grad - row_delta[:, None]) * score_scale).astype(
            jnp.bfloat16
        )
        query_grad = query_grad + jnp.dot(score_grad, key_rows, preferred_element_type=jnp.float32)
        key_grad = lax.dot_general(
            score_grad, query_rows, contract_rows, preferred_element_type=jnp.float32
        )
        value_grad = lax.dot_general(
            probs_half, grad_rows, contract_rows, preferred_element_type=jnp.float32
        )
        key_terms = lax.dynamic_update_slice_in_dim(
            key_terms, jnp.concatenate([key_grad, value_grad], axis=1), offset, 0
        )
        return (query_grad, key_terms)

    initial = (
        jnp.zeros((rows_all, HEAD_DIMENSION), jnp.float32),
        jnp.zeros((total_rows, 2 * HEAD_DIMENSION), jnp.float32),
    )
    query_grad, key_terms = lax.fori_loop(0, needed, backward_step, initial)
    key_value_grad = lax.psum_scatter(key_terms, "seq", scatter_dimension=0, tiled=True).astype(
        jnp.bfloat16
    )
    head_grads = jnp.concatenate(
        [
            query_grad.astype(jnp.bfloat16).reshape(local_rows, QUERY_PER_GROUP * HEAD_DIMENSION),
            key_value_grad,
        ],
        axis=1,
    )
    grad_term = lax.dot_general(
        tokens, head_grads, contract_rows, preferred_element_type=jnp.float32
    )
    normalizing_scale = math.sqrt(
        INPUT_FEATURES * KEY_VALUE_HEADS * (QUERY_PER_GROUP + 2) * HEAD_DIMENSION
    )
    ascent_radius = 0.2 * math.sqrt(KEY_VALUE_HEADS * (QUERY_PER_GROUP + 2) * HEAD_DIMENSION)
    weight_grad = lax.psum(grad_term, "seq")
    square_sum = lax.psum(jnp.sum(weight_grad * weight_grad), "head")
    grad_norm = jnp.sqrt(square_sum)
    share_rows = INPUT_FEATURES // lax.axis_size("seq")
    own_grad = lax.dynamic_slice_in_dim(
        weight_grad, lax.axis_index("seq") * share_rows, share_rows, 0
    )
    direction = own_grad * (normalizing_scale / grad_norm)
    moved_weights = (
        projection.astype(jnp.float32) + ascent_radius / grad_norm * weight_grad
    ).astype(jnp.bfloat16)
    projected_new = jnp.dot(tokens, moved_weights, preferred_element_type=jnp.float32).astype(
        jnp.bfloat16
    )
    query_new, key_value_new = split_heads(projected_new)
    fold_new = attend_fold(query_new, query_pos, score_scale)
    final_state = fold_new(
        empty_state(), lax.all_gather(key_value_new, "seq", axis=0, tiled=True), jnp.int32(0)
    )
    perturbed = (
        (final_state[2] / final_state[1][:, None])
        .astype(jnp.bfloat16)
        .reshape(local_rows, QUERY_PER_GROUP * HEAD_DIMENSION)
    )
    return (perturbed, direction)


def solution(mesh):
    return jax.shard_map(
        on_device,
        mesh=mesh,
        in_specs=(P("seq", None), P(None, "head"), P("seq", "head")),
        out_specs=(P("seq", "head"), P("seq", "head")),
        check_vma=False,
    )
```

profile of v0, /device:TPU:0, one launch (start us, length us, event | category | flops | bytes accessed | tf_op | source)
XLA Modules:
  0.0 397.3 jit_solution(14726550498906386122)
XLA Ops:
  7.2 0.0 reduce-scatter.2.cloned.1.call-start
  7.2 1.0 copy-done
  8.2 2.5 convolution_convert_fusion
  10.7 0.2 copy.21
  10.9 0.1 copy.22
  11.0 33.0 %all_gather.6 = bf16[1024,256]{1,0:T(8,128)(2,1)S(1)} all-gather(bf16[128,256]{1,0:T(8,128)(2,1)S(1)} %copy.22), channel_id=1, replica_groups=mesh['seq'=8,'head'=4] {'seq'}, dimensions={0}, use_global_device_ids=true | all-gather | bytes 589824 | tf_op jit(solution)/shard_map/all_gather | solution.py:75
  44.0 0.1 copy.23
  44.2 1.8 while.46
  44.3 0.3 fusion.107
  44.6 0.2 fusion.108
  44.9 1.2 convolution_add_fusion.6
  46.1 0.1 reshape.57
  46.2 0.2 multiply_reduce_fusion.1
  46.4 1.1 broadcast_in_dim.50
  47.6 2.6 while.47
  47.6 0.4 fusion.120
  48.0 0.3 fusion.121
  48.3 0.3 fusion.123
  48.6 0.3 fusion.122
  48.9 0.9 maximum_dynamic-update-slice_fusion.2
  49.8 0.4 convolution_add_fusion.7
  50.1 0.0 reduce-scatter.2.cloned.1.call-update
  50.2 0.0 all-reduce.2.cloned.1.call-start
  50.2 0.1 reshape.58
  50.3 70.2 %reduce-scatter.2.cloned.1.call-done = f32[128,256]{0,1:T(8,128)} async-done(((f32[1024,256]{0,1:T(8,128)}), f32[128,256]{0,1:T(8,128)}) %reduce-scatter.2.cloned.1.call-update) | async-done | bytes 131088 | tf_op jit(solution)/shard_map/reduce_scatter | solution.py:124
  120.6 0.9 convert_element_type.49
  121.5 0.1 copy.24
  121.6 3.7 convolution_bitcast_fusion
  125.3 0.0 all-reduce.2.cloned.1.call-update
  125.3 4.7 %copy.20 = bf16[2048,768]{0,1:T(8,128)(2,1)} copy(bf16[2048,768]{1,0:T(8,128)(2,1)} %param.10) | data formatting | bytes 6291456 | tf_op args[1]
  130.0 204.6 %all-reduce.2.cloned.1.call-done = f32[2048,768]{0,1:T(8,128)} async-done(((f32[2048,768]{0,1:T(8,128)}), f32[2048,768]{0,1:T(8,128)}) %all-reduce.2.cloned.1.call-update) | async-done | bytes 6291472 | tf_op jit(solution)/shard_map/psum | solution.py:141
  334.6 5.0 %multiply_reduce_fusion = f32[]{:T(128)} fusion(f32[2048,768]{0,1:T(8,128)} %all-reduce.2.cloned.1.call-done), kind=kLoop, calls=%fused_computation.85 | loop fusion | flops 3145727 | bytes 6291460 | tf_op jit(solution)/shard_map/reduce_sum | solution.py:142
  339.6 6.8 %psum.15 = f32[]{:T(128)} all-reduce(f32[]{:T(128)} %multiply_reduce_fusion), channel_id=1, replica_groups=mesh['seq'=8,'head'=4] {'head'}, use_global_device_ids=true, to_apply=%region_10.11 | all-reduce | flops 1 | bytes 8 | tf_op jit(solution)/shard_map/psum | solution.py:142
  347.2 4.7 %fusion.58 = bf16[768,128]{1,0:T(8,128)(2,1)S(1)} fusion(bf16[128,2048]{1,0:T(8,128)(2,1)S(1)} %copy-done, f32[2048,768]{0,1:T(8,128)} %all-reduce.2.cloned.1.call-done, bf16[2048,768]{0,1:T(8,128)(2,1)} %copy.20, f32[]{:T(128)S(6)} %div.45), kind=kOutput, calls=%fused_computation.89 | convolution fusion | flops 409042944 | bytes 10158084 | tf_op jit(solution)/shard_map/dot_general | solution.py:152
  352.0 1.2 dynamic-slice_multiply_fusion
  353.2 1.1 copy.27
  354.3 0.1 copy.28
  354.4 31.3 %all_gather.7 = bf16[1024,256]{1,0:T(8,128)(2,1)S(1)} all-gather(bf16[128,256]{1,0:T(8,128)(2,1)S(1)} %copy.28), channel_id=1, replica_groups=mesh['seq'=8,'head'=4] {'seq'}, dimensions={0}, use_global_device_ids=true | all-gather | bytes 589824 | tf_op jit(solution)/shard_map/all_gather | solution.py:158
  385.8 0.1 copy.26
  385.9 3.6 while.48
  385.9 0.3 fusion.127
  386.3 0.2 fusion.128
  386.5 1.2 convolution_add_fusion.8
  387.7 0.3 fusion.127
  388.1 0.2 fusion.128
  388.3 1.2 convolution_add_fusion.8
  389.5 0.1 divide_convert_fusion
  389.7 0.7 reshape.62
  (29 shorter events, 0.2 us)
Async XLA Ops:
  7.2 1.0 copy-start
  7.2 113.4 %reduce-scatter.2.cloned.1.call-start = ((), (), s32[]{:S(2)}) async-start(), calls=%async_computation.1 | async-start | bytes 1179648 | tf_op jit(solution)/shard_map/reduce_scatter | solution.py:124
  44.2 1.8 copy-start.1
  50.2 284.5 %all-reduce.2.cloned.1.call-start = ((), (), s32[]{:S(2)}) async-start(), calls=%async_computation.2 | async-start | bytes 12582912 | tf_op jit(solution)/shard_map/psum | solution.py:141
Sparse Core Ops, SparseCore 0:
  50.3 70.2 reduce-scatter.1
  125.4 209.1 all-reduce.1
where the time goes:
time: 398 us; the launch traced here: 397 us
  waiting for transfers between devices  275 us (69%)
  blocking collectives  71.2 us (18%)
  matrix products  16.9 us (4%)
  between operations  15 us (4%)
  local copies, waits for them, and re-layouts  9.76 us (2%)
  other arithmetic  9.18 us (2%)
    psum x1, waiting for transfers between devices, on_device(): weight_grad = lax.psum(grad_term, 'seq')  205 us
    reduce_scatter x1, waiting for transfers between devices, on_device(): lax.psum_scatter(key_terms, 'seq', scatter_dimension=0, tiled=True)  70.2 us
    all_gather x1, blocking collectives, on_device(): gathered = lax.all_gather(key_value, 'seq', axis=0, tiled=True)  33 us
    all_gather x1, blocking collectives, on_device(): lax.all_gather(key_value_new, 'seq', axis=0, tiled=True)  31.3 us
  transfers between devices with their start and end apart: 2, of which 2 were waited for; matrix products, arithmetic and copies ran while one was open for 1% of the time, Pallas kernels for 0%

commit v1 on v0

--- a/solution.py
+++ b/solution.py
@@ -138,7 +138,13 @@
         INPUT_FEATURES * KEY_VALUE_HEADS * (QUERY_PER_GROUP + 2) * HEAD_DIMENSION
     )
     ascent_radius = 0.2 * math.sqrt(KEY_VALUE_HEADS * (QUERY_PER_GROUP + 2) * HEAD_DIMENSION)
-    weight_grad = lax.psum(grad_term, "seq")
+    size = lax.axis_size("seq")
+    weight_grad, reach = (grad_term, 1)
+    while reach < size:
+        weight_grad = weight_grad + lax.ppermute(
+            weight_grad, "seq", [(i, i ^ reach) for i in range(size)]
+        )
+        reach = 2 * reach
     square_sum = lax.psum(jnp.sum(weight_grad * weight_grad), "head")
     grad_norm = jnp.sqrt(square_sum)
     share_rows = INPUT_FEATURES // lax.axis_size("seq")

time: 398 us -> 738 us (1.85)
  waiting for transfers between devices: 275 us -> 602 us
  other arithmetic: 9.18 us -> 20.2 us
    ppermute x0 -> x3, waiting for transfers between devices: none -> 532 us  [on_device(): lax.ppermute(weight_grad, 'seq', [(i, i ^ reach) for i in range(size)])]
    psum x1 -> x0, waiting for transfers between devices: 205 us -> none  [on_device(): weight_grad = lax.psum(grad_term, 'seq')]
  transfers between devices with their start and end apart: 2 -> 4, of which waited for: 2 -> 4; matrix products, arithmetic and copies ran while one was open for 1% -> 1% of each run, Pallas kernels for 0% -> 0%
where the time goes in v1:
time: 738 us; the launch traced here: 737 us
  waiting for transfers between devices  602 us (82%)
  blocking collectives  72.1 us (10%)
  other arithmetic  20.2 us (3%)
  between operations  15 us (2%)
  matrix products  14.3 us (2%)
  local copies, waits for them, and re-layouts  9.75 us (1%)
    ppermute x3, waiting for transfers between devices, on_device(): lax.ppermute(weight_grad, 'seq', [(i, i ^ reach) for i in range(size)])  532 us
    reduce_scatter x1, waiting for transfers between devices, on_device(): lax.psum_scatter(key_terms, 'seq', scatter_dimension=0, tiled=True)  70.2 us
    all_gather x1, blocking collectives, on_device(): gathered = lax.all_gather(key_value, 'seq', axis=0, tiled=True)  33 us
    all_gather x1, blocking collectives, on_device(): lax.all_gather(key_value_new, 'seq', axis=0, tiled=True)  31.4 us
  transfers between devices with their start and end apart: 4, of which 4 were waited for; matrix products, arithmetic and copies ran while one was open for 1% of the time, Pallas kernels for 0%

profile of v1, /device:TPU:0, one launch (start us, length us, event | category | flops | bytes accessed | tf_op | source)
XLA Modules:
  0.0 737.2 jit_solution(11627710627217491548)
XLA Ops:
  7.2 1.0 copy-done
  8.2 2.5 convolution_convert_fusion
  10.7 0.2 copy.21
  10.9 0.1 copy.22
  11.0 33.0 %all_gather.6 = bf16[1024,256]{1,0:T(8,128)(2,1)S(1)} all-gather(bf16[128,256]{1,0:T(8,128)(2,1)S(1)} %copy.22), channel_id=1, replica_groups=mesh['seq'=8,'head'=4] {'seq'}, dimensions={0}, use_global_device_ids=true | all-gather | bytes 589824 | tf_op jit(solution)/shard_map/all_gather | solution.py:75
  44.0 0.1 copy.23
  44.2 1.8 while.46
  44.3 0.3 fusion.107
  44.6 0.2 fusion.108
  44.9 1.2 convolution_add_fusion.6
  46.2 0.2 multiply_reduce_fusion.1
  46.4 1.1 broadcast_in_dim.50
  47.6 2.6 while.47
  47.6 0.4 fusion.120
  48.0 0.3 fusion.121
  48.3 0.3 fusion.123
  48.6 0.3 fusion.122
  48.9 0.9 maximum_dynamic-update-slice_fusion.2
  49.8 0.4 convolution_add_fusion.7
  50.3 70.2 %reduce-scatter.2.cloned.1.call-done = f32[128,256]{0,1:T(8,128)} async-done(((f32[1024,256]{0,1:T(8,128)}), f32[128,256]{0,1:T(8,128)}) %reduce-scatter.2.cloned.1.call-update) | async-done | bytes 131088 | tf_op jit(solution)/shard_map/reduce_scatter | solution.py:124
  120.5 0.9 convert_element_type.49
  121.4 0.1 copy.24
  121.6 1.0 convolution_bitcast_fusion
  122.6 1.2 collective-permute-start
  123.7 134.4 %collective-permute-done = f32[2048,768]{0,1:T(8,128)S(1)} collective-permute-done((f32[2048,768]{0,1:T(8,128)S(1)}, f32[2048,768]{0,1:T(8,128)S(1)}, u32[]{:S(2)}, u32[]{:S(2)}) %collective-permute-start) | collective-permute-done | bytes 6291488 | tf_op jit(solution)/shard_map/ppermute | solution.py:144
  258.1 1.9 add.136
  260.0 1.1 collective-permute-start.1
  261.1 133.5 %collective-permute-done.1 = f32[2048,768]{0,1:T(8,128)S(1)} collective-permute-done((f32[2048,768]{0,1:T(8,128)S(1)}, f32[2048,768]{0,1:T(8,128)S(1)}, u32[]{:S(2)}, u32[]{:S(2)}) %collective-permute-start.1) | collective-permute-done | bytes 6291488 | tf_op jit(solution)/shard_map/ppermute | solution.py:144
  394.7 4.0 add.137
  398.6 1.1 collective-permute-start.2
  399.7 4.7 copy.20
  404.4 264.0 %collective-permute-done.2 = f32[2048,768]{0,1:T(8,128)} collective-permute-done((f32[2048,768]{0,1:T(8,128)}, f32[2048,768]{0,1:T(8,128)}, u32[]{:S(2)}, u32[]{:S(2)}) %collective-permute-start.2) | collective-permute-done | bytes 6291488 | tf_op jit(solution)/shard_map/ppermute | solution.py:144
  668.4 10.2 %multiply_reduce_fusion = (f32[]{:T(128)}, f32[2048,768]{0,1:T(8,128)}) fusion(f32[2048,768]{0,1:T(8,128)} %add.137, f32[2048,768]{0,1:T(8,128)} %collective-permute-done.2), kind=kLoop, calls=%fused_computation.85 | loop fusion | flops 4718591 | bytes 18874372 | tf_op jit(solution)/shard_map/reduce_sum | solution.py:148
  678.6 7.7 %psum.7 = f32[]{:T(128)} all-reduce(f32[]{:T(128)} %get-tuple-element.364), channel_id=1, replica_groups=mesh['seq'=8,'head'=4] {'head'}, use_global_device_ids=true, to_apply=%region_9.10 | all-reduce | flops 1 | bytes 8 | tf_op jit(solution)/shard_map/psum | solution.py:148
  687.1 4.7 fusion.58
  691.8 1.2 dynamic-slice_multiply_fusion
  693.0 1.1 copy.27
  694.3 31.4 %all_gather.7 = bf16[1024,256]{1,0:T(8,128)(2,1)S(1)} all-gather(bf16[128,256]{1,0:T(8,128)(2,1)S(1)} %copy.28), channel_id=1, replica_groups=mesh['seq'=8,'head'=4] {'seq'}, dimensions={0}, use_global_device_ids=true | all-gather | bytes 589824 | tf_op jit(solution)/shard_map/all_gather | solution.py:164
  725.7 0.1 copy.26
  725.8 3.6 while.48
  725.9 0.3 fusion.127
  726.2 0.2 fusion.128
  726.5 1.2 convolution_add_fusion.8
  727.7 0.3 fusion.127
  728.0 0.2 fusion.128
  728.3 1.2 convolution_add_fusion.8
  729.4 0.1 divide_convert_fusion
  729.6 0.7 reshape.62
  (34 shorter events, 0.5 us)
Async XLA Ops:
  7.2 1.0 copy-start
  7.2 113.4 %reduce-scatter.2.cloned.1.call-start = ((), (), s32[]{:S(2)}) async-start(), calls=%async_computation.1 | async-start | bytes 1179648 | tf_op jit(solution)/shard_map/reduce_scatter | solution.py:124
  44.2 1.8 copy-start.1
  122.6 135.5 %collective-permute-start = (f32[2048,768]{0,1:T(8,128)S(1)}, f32[2048,768]{0,1:T(8,128)S(1)}, u32[]{:S(2)}, u32[]{:S(2)}) collective-permute-start(f32[2048,768]{0,1:T(8,128)S(1)} %convolution_bitcast_fusion), channel_id=1, source_target_pairs={{0,4},{4,0},{8,12},{12,8},{16,20},{20,16},{24,28},{28,24},{1,5},{5... | collective-permute-start | bytes 18874376 | tf_op jit(solution)/shard_map/ppermute | solution.py:144
  260.0 134.7 %collective-permute-start.1 = (f32[2048,768]{0,1:T(8,128)S(1)}, f32[2048,768]{0,1:T(8,128)S(1)}, u32[]{:S(2)}, u32[]{:S(2)}) collective-permute-start(f32[2048,768]{0,1:T(8,128)S(1)} %add.136), channel_id=1, source_target_pairs={{0,8},{4,12},{8,0},{12,4},{16,24},{20,28},{24,16},{28,20},{1,9},{5... | collective-permute-start | bytes 18874376 | tf_op jit(solution)/shard_map/ppermute | solution.py:144
  398.6 269.8 %collective-permute-start.2 = (f32[2048,768]{0,1:T(8,128)}, f32[2048,768]{0,1:T(8,128)}, u32[]{:S(2)}, u32[]{:S(2)}) collective-permute-start(f32[2048,768]{0,1:T(8,128)} %add.137), channel_id=1, source_target_pairs={{0,16},{4,20},{8,24},{12,28},{16,0},{20,4},{24,8},{28,12},{1,17},{... | collective-permute-start | bytes 18874376 | tf_op jit(solution)/shard_map/ppermute | solution.py:144
Sparse Core Ops, SparseCore 0:
  50.3 70.1 reduce-scatter.1
